TPU v7x, 32 devices: a whole 2x2x4 slice. The times are simulated.
32 devices in a mesh: wide: 8 (over z, x), narrow: 4 (over y, core).
Axes of the slice: x: 2, y: 2, z: 4, core: 2. Of those that a mesh axis runs over, the one named last changes fastest.
Arguments:
- batch: float32 [128, 768], P('wide'), may hold values from -9 to 9
- targets: float32 [128, 512], P(('wide', 'narrow')), may hold values from -6 to 6
- centers: float32 [4096, 768], P(('wide', 'narrow')), may hold values from -9 to 9
- weights: float32 [4096, 512], P(('wide', 'narrow')), may hold values from -6 to 6
Outputs:
- residual: float32 [128, 512], P(('wide', 'narrow'))
- new_weights: float32 [4096, 512], P(('wide', 'narrow'))
All inputs are finite; a program needn't handle non-finite values.
Results may differ from a plain program's by a relative error of at most 0.0001.
Values sent between devices are 32-bit elements; how exact they have to be, the bound alone decides.
No kernel may reach another device: no remote copies, remote signals or barrier semaphores. Data moves between devices by JAX's collectives and lax.ppermute only.
A program may use at most 64 MiB of HBM per device.

v0:
```python
import math

import jax
import jax.numpy as jnp
from jax import lax
from jax.sharding import PartitionSpec as P


def shards(batch, targets, centers, weights):
    local_count = centers.shape[0]
    features = centers.shape[1]
    center_total = local_count * lax.axis_size("wide") * lax.axis_size("narrow")
    pred_scale = 8.0 / math.sqrt(center_total)
    center_norms = jnp.sum(centers * centers, axis=1)
    piece = lax.all_gather(batch, "wide", axis=0, tiled=True)
    row_norms = jnp.sum(piece * piece, axis=1)
    cross = jnp.dot(
        piece, centers.T, precision=lax.Precision.HIGHEST, preferred_element_type=jnp.float32
    )
    kernel = jnp.exp(-(row_norms[:, None] + center_norms[None, :] - 2.0 * cross) / features)
    all_rows = kernel.shape[0]
    partial_value = (
        jnp.dot(
            kernel, weights, precision=lax.Precision.HIGHEST, preferred_element_type=jnp.float32
        )
        * pred_scale
    )
    wide_sums = lax.psum_scatter(partial_value, "wide", scatter_dimension=0, tiled=True)
    own_sums = lax.psum_scatter(wide_sums, "narrow", scatter_dimension=0, tiled=True)
    residual = own_sums - targets
    group_rows = lax.all_gather(residual, "narrow", axis=0, tiled=True)
    residual_all = lax.all_gather(group_rows, "wide", axis=0, tiled=True)
    change = lax.dot_general(
        kernel,
        residual_all,
        (((0,), (0,)), ((), ())),
        precision=lax.Precision.HIGHEST,
        preferred_element_type=jnp.float32,
    )
    new_weights = weights - 32.0 / all_rows * change
    return (residual, new_weights)


def solution(mesh):
    return jax.shard_map(
        shards,
        mesh=mesh,
        in_specs=(
            P("wide", None),
            P(("wide", "narrow"), None),
            P(("wide", "narrow"), None),
            P(("wide", "narrow"), None),
        ),
        out_specs=(P(("wide", "narrow"), None), P(("wide", "narrow"), None)),
        check_vma=False,
    )
```

profile of v0, /device:TPU:0, one launch (start us, length us, event | category | flops | bytes accessed | tf_op | source)
XLA Modules:
  0.0 162.1 jit_solution(10125278434743075146)
XLA Ops:
  7.2 0.0 copy-start.2
  7.2 0.0 reduce-scatter.2.cloned.1.call-start
  7.2 1.1 multiply_reduce_fusion
  8.3 0.0 copy-done.2
  8.3 0.0 copy-start
  8.3 32.9 %all_gather.9 = f32[128,768]{1,0:T(8,128)S(1)} all-gather(f32[16,768]{1,0:T(8,128)S(1)} %copy-done.2), channel_id=1, replica_groups=mesh['wide'=8,'narrow'=4] {'wide'}, dimensions={0}, use_global_device_ids=true | all-gather | bytes 442368 | tf_op jit(solution)/shard_map/all_gather | solution.py:15
  41.3 0.1 multiply_reduce_fusion.1
  41.4 0.0 copy-done
  41.4 0.0 copy-start.1
  41.4 0.5 fusion.4
  41.9 0.4 copy-done.1
  42.3 1.1 convolution_multiply_fusion.1
  43.4 0.0 reduce-scatter.2.cloned.1.call-update
  43.4 0.0 copy-start.5
  43.4 0.6 copy-done.5
  44.1 0.6 dynamic-slice
  45.3 0.0 copy-start.4
  45.3 62.0 %reduce-scatter.2.cloned.1.call-done = f32[16,512]{1,0:T(8,128)} async-done(((f32[128,512]{1,0:T(8,128)}), f32[16,512]{1,0:T(8,128)}) %reduce-scatter.2.cloned.1.call-update) | async-done | bytes 32784 | tf_op jit(solution)/shard_map/reduce_scatter | solution.py:28
  107.3 10.8 %all-reduce = f32[16,512]{1,0:T(8,128)S(1)} all-reduce(f32[16,512]{1,0:T(8,128)} %reduce-scatter.2.cloned.1.call-done), channel_id=3, replica_groups=mesh['wide'=8,'narrow'=4] {'narrow'}, use_global_device_ids=true, to_apply=%region_3.0.clone | all-reduce | flops 8192 | bytes 65536
  118.1 0.0 copy-done.4
  118.1 0.0 copy-start.3
  118.2 5.2 %all-gather = f32[4,4,512]{2,1,0:T(4,128)S(1)} all-gather(f32[1,4,512]{2,1,0:T(4,128)S(1)} %bitcast.8), channel_id=1, replica_groups=mesh['wide'=8,'narrow'=4] {'narrow'}, dimensions={0}, use_global_device_ids=true | all-gather | bytes 40960 | tf_op jit(solution)/shard_map/all_gather | solution.py:31
  123.3 0.0 copy-done.3
  123.4 30.7 %all_gather.11 = f32[128,512]{1,0:T(8,128)S(1)} all-gather(f32[16,512]{1,0:T(8,128)S(1)} %reshape.7), channel_id=1, replica_groups=mesh['wide'=8,'narrow'=4] {'wide'}, dimensions={0}, use_global_device_ids=true | all-gather | bytes 294912 | tf_op jit(solution)/shard_map/all_gather | solution.py:32
  154.1 1.1 fusion
  (2 shorter events, 0.0 us)
Async XLA Ops:
  7.2 1.2 copy-start.2
  7.2 100.1 %reduce-scatter.2.cloned.1.call-start = ((), (), s32[]{:S(2)}) async-start(), calls=%async_computation.1 | async-start | bytes 294912 | tf_op jit(solution)/shard_map/reduce_scatter | solution.py:28
  8.3 33.0 %copy-start = (f32[128,768]{1,0:T(8,128)S(1)}, f32[128,768]{1,0:T(8,128)}, u32[]{:S(2)}) copy-start(f32[128,768]{1,0:T(8,128)} %param.6) | copy-start | bytes 1179652
  41.4 1.0 copy-start.1
  43.4 0.7 copy-start.5
  45.3 72.8 %copy-start.4 = (f32[4,512]{1,0:T(4,128)S(1)}, f32[4,512]{1,0:T(4,128)}, u32[]{:S(2)}) copy-start(f32[4,512]{1,0:T(4,128)} %param.5) | copy-start | bytes 24580
  118.1 5.2 %copy-start.3 = (f32[4,512]{1,0:T(4,128)}, f32[4,512]{1,0:T(4,128)S(1)}, u32[]{:S(2)}) copy-start(f32[4,512]{1,0:T(4,128)S(1)} %dynamic-slice_subtract_fusion) | copy-start | bytes 24580
Sparse Core Ops, SparseCore 0:
  43.5 63.7 reduce-scatter.1
where the time goes:
time: 162 us
  blocking collectives  79.6 us (49%)
  waiting for transfers between devices  62 us (38%)
  between operations  14.8 us (9%)
  matrix products  2.69 us (2%)
  local copies, waits for them, and re-layouts  1.72 us (1%)
    reduce_scatter x1, waiting for transfers between devices, shards(): lax.psum_scatter(partial_value, 'wide', scatter_dimension=0, tiled=True)  62 us
    all_gather x1, blocking collectives, shards(): piece = lax.all_gather(batch, 'wide', axis=0, tiled=True)  32.9 us
    all_gather x1, blocking collectives, shards(): residual_all = lax.all_gather(group_rows, 'wide', axis=0, tiled=True)  30.7 us
    unnamed x1, blocking collectives  10.8 us
    all_gather x1, blocking collectives, shards(): group_rows = lax.all_gather(residual, 'narrow', axis=0, tiled=True)  5.19 us
  transfers between devices with their start and end apart: 1, of which 1 were waited for; matrix products, arithmetic and copies ran while one was open for 0% of the time, Pallas kernels for 0%

commit v1 on v0

v1 whole, which is shorter than its diff:
```python
import math

import jax
import jax.numpy as jnp
from jax import lax
from jax.sharding import PartitionSpec as P

AXES = ("wide", "narrow")
HIGHEST = lax.Precision.HIGHEST


def bits_of(size):
    return tuple(1 << b for b in reversed(range(size.bit_length() - 1)))


def swap(value, total, mask):
    pairs = [(i, i ^ mask) for i in range(total)]
    return lax.ppermute(value, AXES, pairs)


def shards(batch, targets, centers, weights):
    wide = lax.axis_size("wide")
    narrow = lax.axis_size("narrow")
    total = wide * narrow
    features = centers.shape[1]
    own_rows = targets.shape[0]
    outputs = targets.shape[1]
    all_rows = own_rows * total
    pred_scale = 8.0 / math.sqrt(centers.shape[0] * total)
    spot = lax.axis_index("narrow")
    lane, seat = spot % 2, spot // 2
    seats = narrow // 2

    paired = batch.reshape(seats, 2, own_rows, features)
    rows = jnp.where(lane == 0, paired[:, 0], paired[:, 1]).reshape(seats * own_rows, features)
    other_centers = swap(centers, total, 1)
    other_weights = swap(weights, total, 1)

    for bit in bits_of(wide):
        rows = jnp.concatenate([rows, swap(rows, total, bit * narrow)], axis=0)

    row_norms = jnp.sum(rows * rows, axis=1)

    def block(points):
        norms = jnp.sum(points * points, axis=1)
        cross = jnp.dot(rows, points.T, precision=HIGHEST, preferred_element_type=jnp.float32)
        return jnp.exp(-(row_norms[:, None] + norms[None, :] - 2.0 * cross) / features)

    def product(kernel, values):
        return jnp.dot(kernel, values, precision=HIGHEST, preferred_element_type=jnp.float32)

    kernel_own = block(centers)
    kernel_other = block(other_centers)
    kernel_swapped = swap(kernel_other, total, 1)
    value = (product(kernel_own, weights) + product(kernel_other, other_weights)) * pred_scale

    lead = seats * own_rows
    mine = (jnp.arange(lead) // own_rows == seat)[:, None]
    taken = jnp.where(mine, jnp.tile(targets, (seats, 1)), 0.0)
    value = jnp.concatenate([value[:lead] - taken, value[lead:]], axis=0)

    half = value.shape[0] // 2
    value = value[:half] + swap(value[half:], total, narrow)
    for mask in bits_of(narrow)[:-1]:
        value = value + swap(value, total, mask)
    count = wide // 2
    for bit in reversed(bits_of(wide)[:-1]):
        other = swap(value, total, bit * narrow)
        slow = bit // 2
        fast = count // (2 * slow)
        other = other.reshape(slow, 2, fast, lead, outputs)[:, ::-1].reshape(value.shape)
        value = value + other
    residual = lax.dynamic_slice_in_dim(value, seat * own_rows, own_rows, axis=0)
    value = jnp.concatenate([value, swap(value, total, narrow)], axis=0)
    other_value = swap(value, total, 1)

    def turned(kernel, values):
        return lax.dot_general(
            kernel, values, (((0,), (0,)), ((), ())), precision=HIGHEST, preferred_element_type=jnp.float32
        )

    change = turned(kernel_own, value) + turned(kernel_swapped, other_value)
    new_weights = weights - 32.0 / all_rows * change
    return (residual, new_weights)


def solution(mesh):
    return jax.shard_map(
        shards,
        mesh=mesh,
        in_specs=(
            P("wide", None),
            P(("wide", "narrow"), None),
            P(("wide", "narrow"), None),
            P(("wide", "narrow"), None),
        ),
        out_specs=(P(("wide", "narrow"), None), P(("wide", "narrow"), None)),
        check_vma=False,
    )
```

time: 162 us -> 44.5 us (0.27)
  blocking collectives: 79.6 us -> 0 us
  waiting for transfers between devices: 62 us -> 16.7 us
  starting transfers between devices: 0.04 us -> 20.1 us
  between operations: 14.8 us -> 0.84 us
    all_gather x3 -> x0, blocking collectives: 68.8 us -> none  [the longest x1 32.9 us: shards(): piece = lax.all_gather(batch, 'wide', axis=0, tiled=True)]
    reduce_scatter x1 -> x0, waiting for transfers between devices: 62 us -> none  [shards(): lax.psum_scatter(partial_value, 'wide', scatter_dimension=0, tiled=True)]
    ppermute x0 -> x12, starting transfers between devices: none -> 20.1 us  [swap(): return lax.ppermute(value, AXES, pairs)]
    ppermute x0 -> x12, waiting for transfers between devices: none -> 16.7 us  [swap(): return lax.ppermute(value, AXES, pairs)]
    unnamed x1 -> x0, blocking collectives: 10.8 us -> none
    dot_general x3 -> x6, matrix products: 2.69 us -> 3.32 us  [the longest x2 1.63 us: turned(): lax.dot_general(kernel, values, (((0,), (0,)), ((), ())), precision=HIGHE...]
  transfers between devices with their start and end apart: 1 -> 12, of which waited for: 1 -> 9; matrix products, arithmetic and copies ran while one was open for 0% -> 8% of each run, Pallas kernels for 0% -> 0%
where the time goes in v1:
time: 44.5 us; the launch traced here: 44.3 us
  starting transfers between devices  20.1 us (45%)
  waiting for transfers between devices  16.7 us (38%)
  matrix products  3.32 us (7%)
  local copies, waits for them, and re-layouts  1.79 us (4%)
  other arithmetic  1.5 us (3%)
  between operations  0.84 us (2%)
    ppermute x12, starting transfers between devices, swap(): return lax.ppermute(value, AXES, pairs)  20.1 us
    ppermute x12, waiting for transfers between devices, swap(): return lax.ppermute(value, AXES, pairs)  16.7 us
    dot_general x2, matrix products, turned(): lax.dot_general(kernel, values, (((0,), (0,)), ((), ())), precision=HIGHE...  1.63 us
    reduce_sum x2, other arithmetic, block(): norms = jnp.sum(points * points, axis=1)  1.23 us
    dot_general x2, matrix products, block(): jnp.dot(rows, points.T, precision=HIGHEST, preferred_element_type=jnp.flo...  1.09 us
  transfers between devices with their start and end apart: 12, of which 9 were waited for; matrix products, arithmetic and copies ran while one was open for 8% of the time, Pallas kernels for 0%

profile of v1, /device:TPU:0, one launch (start us, length us, event | category | flops | bytes accessed | tf_op | source)
XLA Modules:
  0.0 44.3 jit_solution(15429347915979646425)
XLA Ops:
  0.6 0.8 %reshape.45 = f32[2,2,4,768]{3,2,1,0:T(4,128)S(1)} reshape(f32[16,768]{1,0:T(8,128)} %param.4) | data formatting | bytes 98304 | tf_op jit(solution)/shard_map/reshape | solution.py:34
  1.5 4.1 %collective-permute-start = (f32[8,768]{1,0:T(8,128)S(1)}, f32[8,768]{1,0:T(8,128)S(1)}, u32[]{:S(2)}, u32[]{:S(2)}) collective-permute-start(f32[8,768]{1,0:T(8,128)S(1)} %select_n.42), channel_id=1, source_target_pairs={{0,16},{1,17},{2,18},{3,19},{4,20},{5,21},{6,22},{7,23},{8,24},{9,... | collective-permute-start | bytes 73736 | tf_op jit(solution)/shard_map/ppermute | solution.py:18
  5.6 0.0 collective-permute-start.3
  5.6 0.5 %collective-permute-start.4 = (f32[128,512]{1,0:T(8,128)}, f32[128,512]{1,0:T(8,128)S(1)}, u32[]{:S(2)}, u32[]{:S(2)}) collective-permute-start(f32[128,512]{1,0:T(8,128)} %param.7), channel_id=1, source_target_pairs={{0,1},{1,0},{2,3},{3,2},{4,5},{5,4},{6,7},{7,6},{8,9},{9,8},{10,11... | collective-permute-start | bytes 786440 | tf_op jit(solution)/shard_map/ppermute | solution.py:18
  6.1 0.0 copy-start.2
  6.1 1.1 %multiply_reduce_fusion.1 = f32[128]{0:T(128)S(1)} fusion(f32[128,768]{1,0:T(8,128)} %param.6), kind=kLoop, calls=%fused_computation.8 | loop fusion | flops 196480 | bytes 393728 | tf_op jit(solution)/shard_map/reduce_sum | solution.py:45
  7.3 0.0 copy-start
  7.3 0.0 copy-done.2
  7.3 0.1 collective-permute-done
  7.5 1.9 %collective-permute-start.1 = (f32[16,768]{1,0:T(8,128)S(1)}, f32[16,768]{1,0:T(8,128)S(1)}, u32[]{:S(2)}, u32[]{:S(2)}) collective-permute-start(f32[16,768]{1,0:T(8,128)S(1)} %pad_maximum_fusion.3), channel_id=1, source_target_pairs={{0,8},{1,9},{2,10},{3,11},{4,12},{5,13},{6,14},{7,15},{8,0},{9,1},... | collective-permute-start | bytes 147464 | tf_op jit(solution)/shard_map/ppermute | solution.py:18
  9.4 2.2 %collective-permute-done.1 = f32[16,768]{1,0:T(8,128)S(1)} collective-permute-done((f32[16,768]{1,0:T(8,128)S(1)}, f32[16,768]{1,0:T(8,128)S(1)}, u32[]{:S(2)}, u32[]{:S(2)}) %collective-permute-start.1) | collective-permute-done | bytes 49184 | tf_op jit(solution)/shard_map/ppermute | solution.py:18
  11.6 2.0 %collective-permute-start.2 = (f32[32,768]{1,0:T(8,128)S(1)}, f32[32,768]{1,0:T(8,128)S(1)}, u32[]{:S(2)}, u32[]{:S(2)}) collective-permute-start(f32[32,768]{1,0:T(8,128)S(1)} %pad_maximum_fusion.1), channel_id=1, source_target_pairs={{0,4},{1,5},{2,6},{3,7},{4,0},{5,1},{6,2},{7,3},{8,12},{9,13},{10,... | collective-permute-start | bytes 294920 | tf_op jit(solution)/shard_map/ppermute | solution.py:18
  13.6 2.7 %collective-permute-done.2 = f32[32,768]{1,0:T(8,128)S(1)} collective-permute-done((f32[32,768]{1,0:T(8,128)S(1)}, f32[32,768]{1,0:T(8,128)S(1)}, u32[]{:S(2)}, u32[]{:S(2)}) %collective-permute-start.2) | collective-permute-done | bytes 98336 | tf_op jit(solution)/shard_map/ppermute | solution.py:18
  16.2 0.0 copy-done
  16.3 0.0 copy-start.1
  16.3 0.5 %convolution_multiply_fusion.1 = f32[64,128]{1,0:T(8,128)S(1)} fusion(f32[64,768]{1,0:T(8,128)S(1)} %constant_dynamic-update-slice_fusion, f32[128,768]{1,0:T(8,128)S(1)} %copy-done), kind=kOutput, calls=%fused_computation.6 | convolution fusion | flops 75505664 | bytes 622592 | tf_op jit(solution)/shard_map/dot_general | solution.py:46
  16.8 0.1 multiply_reduce_fusion.2
  16.9 0.3 copy-done.1
  17.2 0.3 fusion.4
  17.5 0.0 collective-permute-done.3
  17.6 0.1 multiply_reduce_fusion
  17.7 0.6 %multiply_exponential_fusion = f32[64,128]{1,0:T(8,128)S(1)} fusion(f32[128]{0:T(128)S(1)} %multiply_reduce_fusion, f32[64,768]{1,0:T(8,128)S(1)} %constant_dynamic-update-slice_fusion, f32[128,768]{1,0:T(8,128)S(1)} %collective-permute-done.3, f32[64]{0:T(128)S(1)} %multiply_reduce_fusion.2), kind=kOutput, calls=%fused_computation.17 | convolution fusion | flops 75538432 | bytes 623360 | tf_op jit(solution)/shard_map/dot_general | solution.py:46
  18.2 0.0 collective-permute-done.4
  18.2 0.3 fusion.2
  18.5 2.0 %collective-permute-start.5 = (f32[32,512]{1,0:T(8,128)S(1)}, f32[32,512]{1,0:T(8,128)S(1)}, u32[]{:S(2)}, u32[]{:S(2)}) collective-permute-start(f32[32,512]{1,0:T(8,128)S(1)} %slice.29), channel_id=1, source_target_pairs={{0,4},{1,5},{2,6},{3,7},{4,0},{5,1},{6,2},{7,3},{8,12},{9,13},{10,... | collective-permute-start | bytes 196616 | tf_op jit(solution)/shard_map/ppermute | solution.py:18
  20.5 0.1 slice_subtract_fusion
  20.6 2.2 %collective-permute-done.5 = f32[32,512]{1,0:T(8,128)S(1)} collective-permute-done((f32[32,512]{1,0:T(8,128)S(1)}, f32[32,512]{1,0:T(8,128)S(1)}, u32[]{:S(2)}, u32[]{:S(2)}) %collective-permute-start.5) | collective-permute-done | bytes 65568 | tf_op jit(solution)/shard_map/ppermute | solution.py:18
  22.9 2.0 %collective-permute-start.6 = (f32[32,512]{1,0:T(8,128)S(1)}, f32[32,512]{1,0:T(8,128)S(1)}, u32[]{:S(2)}, u32[]{:S(2)}) collective-permute-start(f32[32,512]{1,0:T(8,128)S(1)} %fusion.3), channel_id=1, source_target_pairs={{0,2},{1,3},{2,0},{3,1},{4,6},{5,7},{6,4},{7,5},{8,10},{9,11},{10,... | collective-permute-start | bytes 196616 | tf_op jit(solution)/shard_map/ppermute | solution.py:18
  24.9 2.3 %collective-permute-done.6 = f32[32,512]{1,0:T(8,128)S(1)} collective-permute-done((f32[32,512]{1,0:T(8,128)S(1)}, f32[32,512]{1,0:T(8,128)S(1)}, u32[]{:S(2)}, u32[]{:S(2)}) %collective-permute-start.6) | collective-permute-done | bytes 65568 | tf_op jit(solution)/shard_map/ppermute | solution.py:18
  27.2 2.0 %collective-permute-start.7 = (f32[32,512]{1,0:T(8,128)S(1)}, f32[32,512]{1,0:T(8,128)S(1)}, u32[]{:S(2)}, u32[]{:S(2)}) collective-permute-start(f32[32,512]{1,0:T(8,128)S(1)} %add.63), channel_id=1, source_target_pairs={{0,8},{1,9},{2,10},{3,11},{4,12},{5,13},{6,14},{7,15},{8,0},{9,1},... | collective-permute-start | bytes 196616 | tf_op jit(solution)/shard_map/ppermute | solution.py:18
  29.2 2.4 %collective-permute-done.7 = f32[32,512]{1,0:T(8,128)S(1)} collective-permute-done((f32[32,512]{1,0:T(8,128)S(1)}, f32[32,512]{1,0:T(8,128)S(1)}, u32[]{:S(2)}, u32[]{:S(2)}) %collective-permute-start.7) | collective-permute-done | bytes 65568 | tf_op jit(solution)/shard_map/ppermute | solution.py:18
  31.6 3.0 %collective-permute-start.8 = (f32[32,512]{1,0:T(8,128)S(1)}, f32[32,512]{1,0:T(8,128)S(1)}, u32[]{:S(2)}, u32[]{:S(2)}) collective-permute-start(f32[32,512]{1,0:T(8,128)S(1)} %bitcast_add_fusion.1), channel_id=1, source_target_pairs={{0,16},{1,17},{2,18},{3,19},{4,20},{5,21},{6,22},{7,23},{8,24},{9,... | collective-permute-start | bytes 196616 | tf_op jit(solution)/shard_map/ppermute | solution.py:18
  34.6 2.2 %collective-permute-done.8 = f32[32,512]{1,0:T(8,128)S(1)} collective-permute-done((f32[32,512]{1,0:T(8,128)S(1)}, f32[32,512]{1,0:T(8,128)S(1)}, u32[]{:S(2)}, u32[]{:S(2)}) %collective-permute-start.8) | collective-permute-done | bytes 65568 | tf_op jit(solution)/shard_map/ppermute | solution.py:18
  36.8 2.0 %collective-permute-start.9 = (f32[32,512]{1,0:T(8,128)S(1)}, f32[32,512]{1,0:T(8,128)S(1)}, u32[]{:S(2)}, u32[]{:S(2)}) collective-permute-start(f32[32,512]{1,0:T(8,128)S(1)} %bitcast_add_fusion), channel_id=1, source_target_pairs={{0,4},{1,5},{2,6},{3,7},{4,0},{5,1},{6,2},{7,3},{8,12},{9,13},{10,... | collective-permute-start | bytes 196616 | tf_op jit(solution)/shard_map/ppermute | solution.py:18
  38.8 2.3 %collective-permute-done.9 = f32[32,512]{1,0:T(8,128)S(1)} collective-permute-done((f32[32,512]{1,0:T(8,128)S(1)}, f32[32,512]{1,0:T(8,128)S(1)}, u32[]{:S(2)}, u32[]{:S(2)}) %collective-permute-start.9) | collective-permute-done | bytes 65568 | tf_op jit(solution)/shard_map/ppermute | solution.py:18
  41.2 0.1 collective-permute-start.11
  41.2 0.5 %collective-permute-start.10 = (f32[64,128]{1,0:T(8,128)S(1)}, f32[64,128]{1,0:T(8,128)S(1)}, u32[]{:S(2)}, u32[]{:S(2)}) collective-permute-start(f32[64,128]{1,0:T(8,128)S(1)} %multiply_exponential_fusion), channel_id=1, source_target_pairs={{0,1},{1,0},{2,3},{3,2},{4,5},{5,4},{6,7},{7,6},{8,9},{9,8},{10,11... | collective-permute-start | bytes 98312 | tf_op jit(solution)/shard_map/ppermute | solution.py:18
  41.7 0.6 %constant_dynamic-slice_fusion = f32[4,512]{1,0:T(4,128)} fusion(f32[32,512]{1,0:T(8,128)S(1)} %bitcast_add_fusion, s32[]{:T(128)S(6)} %select_n.46), kind=kLoop, calls=%fused_computation.37 | loop fusion | bytes 16388 | tf_op jit(solution)/shard_map/dynamic_slice | solution.py:73
  42.3 0.3 collective-permute-done.10
  42.6 0.0 collective-permute-done.11
  42.6 0.4 fusion.14
  43.0 1.2 %fusion.1 = f32[128,512]{1,0:T(8,128)} fusion(f32[128,512]{1,0:T(8,128)S(1)} %copy-done.1, f32[128,512]{1,0:T(8,128)S(1)} %fusion.14, f32[64,128]{1,0:T(8,128)S(1)} %convolution_multiply_fusion.1, f32[128]{0:T(128)S(1)} %multiply_reduce_fusion.1, f32[64]{0:T(128)S(1)} %multiply_reduce_fusion.2, f32[32,512]{1,0:T(8,128)S(1)} %collective-permute-done.9, ...), kind=kOutput, calls=%fused_computation.2 | convolution fusion | flops 50593792 | bytes 951040 | tf_op jit(solution)/shard_map/dot_general | solution.py:78
  (20 shorter events, 0.2 us)
Async XLA Ops:
  1.5 5.9 %collective-permute-start = (f32[8,768]{1,0:T(8,128)S(1)}, f32[8,768]{1,0:T(8,128)S(1)}, u32[]{:S(2)}, u32[]{:S(2)}) collective-permute-start(f32[8,768]{1,0:T(8,128)S(1)} %select_n.42), channel_id=1, source_target_pairs={{0,16},{1,17},{2,18},{3,19},{4,20},{5,21},{6,22},{7,23},{8,24},{9,... | collective-permute-start | bytes 73736 | tf_op jit(solution)/shard_map/ppermute | solution.py:18
  5.6 11.9 %collective-permute-start.3 = (f32[128,768]{1,0:T(8,128)}, f32[128,768]{1,0:T(8,128)S(1)}, u32[]{:S(2)}, u32[]{:S(2)}) collective-permute-start(f32[128,768]{1,0:T(8,128)} %param.6), channel_id=1, source_target_pairs={{0,1},{1,0},{2,3},{3,2},{4,5},{5,4},{6,7},{7,6},{8,9},{9,8},{10,11... | collective-permute-start | bytes 1179656 | tf_op jit(solution)/shard_map/ppermute | solution.py:18
  5.6 12.6 %collective-permute-start.4 = (f32[128,512]{1,0:T(8,128)}, f32[128,512]{1,0:T(8,128)S(1)}, u32[]{:S(2)}, u32[]{:S(2)}) collective-permute-start(f32[128,512]{1,0:T(8,128)} %param.7), channel_id=1, source_target_pairs={{0,1},{1,0},{2,3},{3,2},{4,5},{5,4},{6,7},{7,6},{8,9},{9,8},{10,11... | collective-permute-start | bytes 786440 | tf_op jit(solution)/shard_map/ppermute | solution.py:18
  6.1 1.2 %copy-start.2 = (f32[4,512]{1,0:T(4,128)S(1)}, f32[4,512]{1,0:T(4,128)}, u32[]{:S(2)}) copy-start(f32[4,512]{1,0:T(4,128)} %param.5) | copy-start | bytes 24580
  7.3 9.0 %copy-start = (f32[128,768]{1,0:T(8,128)S(1)}, f32[128,768]{1,0:T(8,128)}, u32[]{:S(2)}) copy-start(f32[128,768]{1,0:T(8,128)} %param.6) | copy-start | bytes 1179652
  7.5 4.1 %collective-permute-start.1 = (f32[16,768]{1,0:T(8,128)S(1)}, f32[16,768]{1,0:T(8,128)S(1)}, u32[]{:S(2)}, u32[]{:S(2)}) collective-permute-start(f32[16,768]{1,0:T(8,128)S(1)} %pad_maximum_fusion.3), channel_id=1, source_target_pairs={{0,8},{1,9},{2,10},{3,11},{4,12},{5,13},{6,14},{7,15},{8,0},{9,1},... | collective-permute-start | bytes 147464 | tf_op jit(solution)/shard_map/ppermute | solution.py:18
  11.6 4.7 %collective-permute-start.2 = (f32[32,768]{1,0:T(8,128)S(1)}, f32[32,768]{1,0:T(8,128)S(1)}, u32[]{:S(2)}, u32[]{:S(2)}) collective-permute-start(f32[32,768]{1,0:T(8,128)S(1)} %pad_maximum_fusion.1), channel_id=1, source_target_pairs={{0,4},{1,5},{2,6},{3,7},{4,0},{5,1},{6,2},{7,3},{8,12},{9,13},{10,... | collective-permute-start | bytes 294920 | tf_op jit(solution)/shard_map/ppermute | solution.py:18
  16.3 1.0 %copy-start.1 = (f32[128,512]{1,0:T(8,128)S(1)}, f32[128,512]{1,0:T(8,128)}, u32[]{:S(2)}) copy-start(f32[128,512]{1,0:T(8,128)} %param.7) | copy-start | bytes 786436
  18.5 4.3 %collective-permute-start.5 = (f32[32,512]{1,0:T(8,128)S(1)}, f32[32,512]{1,0:T(8,128)S(1)}, u32[]{:S(2)}, u32[]{:S(2)}) collective-permute-start(f32[32,512]{1,0:T(8,128)S(1)} %slice.29), channel_id=1, source_target_pairs={{0,4},{1,5},{2,6},{3,7},{4,0},{5,1},{6,2},{7,3},{8,12},{9,13},{10,... | collective-permute-start | bytes 196616 | tf_op jit(solution)/shard_map/ppermute | solution.py:18
  22.9 4.3 %collective-permute-start.6 = (f32[32,512]{1,0:T(8,128)S(1)}, f32[32,512]{1,0:T(8,128)S(1)}, u32[]{:S(2)}, u32[]{:S(2)}) collective-permute-start(f32[32,512]{1,0:T(8,128)S(1)} %fusion.3), channel_id=1, source_target_pairs={{0,2},{1,3},{2,0},{3,1},{4,6},{5,7},{6,4},{7,5},{8,10},{9,11},{10,... | collective-permute-start | bytes 196616 | tf_op jit(solution)/shard_map/ppermute | solution.py:18
  27.2 4.3 %collective-permute-start.7 = (f32[32,512]{1,0:T(8,128)S(1)}, f32[32,512]{1,0:T(8,128)S(1)}, u32[]{:S(2)}, u32[]{:S(2)}) collective-permute-start(f32[32,512]{1,0:T(8,128)S(1)} %add.63), channel_id=1, source_target_pairs={{0,8},{1,9},{2,10},{3,11},{4,12},{5,13},{6,14},{7,15},{8,0},{9,1},... | collective-permute-start | bytes 196616 | tf_op jit(solution)/shard_map/ppermute | solution.py:18
  31.6 5.2 %collective-permute-start.8 = (f32[32,512]{1,0:T(8,128)S(1)}, f32[32,512]{1,0:T(8,128)S(1)}, u32[]{:S(2)}, u32[]{:S(2)}) collective-permute-start(f32[32,512]{1,0:T(8,128)S(1)} %bitcast_add_fusion.1), channel_id=1, source_target_pairs={{0,16},{1,17},{2,18},{3,19},{4,20},{5,21},{6,22},{7,23},{8,24},{9,... | collective-permute-start | bytes 196616 | tf_op jit(solution)/shard_map/ppermute | solution.py:18
  36.8 4.3 %collective-permute-start.9 = (f32[32,512]{1,0:T(8,128)S(1)}, f32[32,512]{1,0:T(8,128)S(1)}, u32[]{:S(2)}, u32[]{:S(2)}) collective-permute-start(f32[32,512]{1,0:T(8,128)S(1)} %bitcast_add_fusion), channel_id=1, source_target_pairs={{0,4},{1,5},{2,6},{3,7},{4,0},{5,1},{6,2},{7,3},{8,12},{9,13},{10,... | collective-permute-start | bytes 196616 | tf_op jit(solution)/shard_map/ppermute | solution.py:18
  41.2 1.5 %collective-permute-start.11 = (f32[64,512]{1,0:T(8,128)S(1)}, f32[64,512]{1,0:T(8,128)S(1)}, u32[]{:S(2)}, u32[]{:S(2)}) collective-permute-start(f32[64,512]{1,0:T(8,128)S(1)} %pad_maximum_fusion), channel_id=1, source_target_pairs={{0,1},{1,0},{2,3},{3,2},{4,5},{5,4},{6,7},{7,6},{8,9},{9,8},{10,11... | collective-permute-start | bytes 393224 | tf_op jit(solution)/shard_map/ppermute | solution.py:18
  41.2 1.4 %collective-permute-start.10 = (f32[64,128]{1,0:T(8,128)S(1)}, f32[64,128]{1,0:T(8,128)S(1)}, u32[]{:S(2)}, u32[]{:S(2)}) collective-permute-start(f32[64,128]{1,0:T(8,128)S(1)} %multiply_exponential_fusion), channel_id=1, source_target_pairs={{0,1},{1,0},{2,3},{3,2},{4,5},{5,4},{6,7},{7,6},{8,9},{9,8},{10,11... | collective-permute-start | bytes 98312 | tf_op jit(solution)/shard_map/ppermute | solution.py:18

commit v2 on v1

v2 whole, which is shorter than its diff:
```python
import functools
import math

import jax
import jax.numpy as jnp
from jax import lax
from jax.experimental import pallas as pl
from jax.experimental.pallas import tpu as pltpu
from jax.sharding import PartitionSpec as P

AXES = ("wide", "narrow")
HIGHEST = lax.Precision.HIGHEST


def odd(number):
    return number.bit_count() % 2


def swap(value, total, masks):
    return lax.ppermute(value, AXES, [(i, i ^ masks[odd(i)]) for i in range(total)])


def flipped(value, place, lead):
    if place is None:
        return value
    shape = (-1, 2, lead << place, value.shape[1])
    return value.reshape(shape)[:, ::-1].reshape(value.shape)


def contract(left, right, dims):
    return lax.dot_general(
        left, right, (dims, ((), ())), precision=HIGHEST, preferred_element_type=jnp.float32
    )


def kernel_columns(rows, points, norms):
    row_norms = jnp.sum(rows * rows, axis=1, keepdims=True)
    cross = contract(rows, points, ((1,), (1,)))
    return jnp.exp(-(row_norms + norms - 2.0 * cross) / rows.shape[1])


def early_body(scale, rows, taken, centers, other_centers, weights, other_weights, value, kernel, norms):
    count = centers.shape[0]
    total = None
    for i, (points, gains) in enumerate(((centers, weights), (other_centers, other_weights))):
        squares = points[...] * points[...]
        norm = contract(jnp.ones((8, squares.shape[1]), jnp.float32), squares, ((1,), (1,)))[:1]
        norms[:, i * count : (i + 1) * count] = norm
        block = kernel_columns(rows[...], points[...], norm)
        kernel[:, i * count : (i + 1) * count] = block
        part = contract(block, gains[...], ((1,), (0,)))
        total = part if total is None else total + part
    lead = taken.shape[0]
    value[...] = total * scale
    value[:lead] = value[:lead] - taken[...]


def late_body(
    scale, rows, early, early_kernel, norms, centers, other_centers, weights, other_weights, value, kernel, other_kernel
):
    count = centers.shape[0]
    half = early.shape[0]
    value[:half] = early[...]
    kernel[:half] = early_kernel[:, :count]
    other_kernel[:half] = early_kernel[:, count:]
    own = kernel_columns(rows[...], centers[...], norms[:, :count])
    other = kernel_columns(rows[...], other_centers[...], norms[:, count:])
    kernel[half:] = own
    other_kernel[half:] = other
    value[half:] = (
        contract(own, weights[...], ((1,), (0,))) + contract(other, other_weights[...], ((1,), (0,)))
    ) * scale


def call(body, outs, *operands):
    return pl.pallas_call(
        body,
        out_shape=[jax.ShapeDtypeStruct(shape, jnp.float32) for shape in outs],
        in_specs=[pl.BlockSpec(memory_space=pltpu.VMEM)] * len(operands),
        out_specs=[pl.BlockSpec(memory_space=pltpu.VMEM)] * len(outs),
        compiler_params=pltpu.CompilerParams(vmem_limit_bytes=LIMIT),
    )(*operands)


LIMIT = 24 * 1024 * 1024


def early_half(rows, taken, scale, centers, other_centers, weights, other_weights):
    half, count, width = rows.shape[0], centers.shape[0], weights.shape[1]
    outs = ((half, width), (half, 2 * count), (1, 2 * count))
    return call(
        functools.partial(early_body, scale), outs, rows, taken, centers, other_centers, weights, other_weights
    )


def late_half(rows, early, early_kernel, norms, scale, centers, other_centers, weights, other_weights):
    half, count, width = rows.shape[0], centers.shape[0], weights.shape[1]
    outs = ((2 * half, width), (2 * half, count), (2 * half, count))
    return call(
        functools.partial(late_body, scale),
        outs, rows, early, early_kernel, norms, centers, other_centers, weights, other_weights,
    )


def shards(batch, targets, centers, weights):
    wide = lax.axis_size("wide")
    narrow = lax.axis_size("narrow")
    total = wide * narrow
    features = centers.shape[1]
    own_rows = targets.shape[0]
    own_count = centers.shape[0]
    all_rows = own_rows * total
    pred_scale = 8.0 / math.sqrt(own_count * total)
    spot = lax.axis_index("narrow")
    lane, seat = spot % 2, spot // 2
    seats = narrow // 2
    lead = seats * own_rows
    place = lax.axis_index(AXES)
    parity = sum((place >> b) & 1 for b in range(total.bit_length() - 1)) % 2

    bits = [narrow << b for b in range(wide.bit_length() - 1)]
    first = [bits[0]] + bits[:0:-1]
    second = first[1:] + first[:1]
    spread = list(zip(first, second))
    line = [2 << b for b in range(seats.bit_length() - 1)] + first[1:2] + first[:1] + first[2:]
    other_line = list(line)
    for i in range(0, len(line) - 1, 2):
        other_line[i : i + 2] = line[i + 1], line[i]
    core = (1, 1)

    def across(value, pair):
        return swap(value, total, (pair[0] ^ 1, pair[1] ^ 1))

    def chosen(block, sign):
        pieces = []
        for s in range(seats):
            start = 2 * s * own_rows
            low, high = block[start : start + own_rows], block[start + own_rows : start + 2 * own_rows]
            want = (lane + sign + sum((s ^ seat) >> b & 1 for b in range(seats.bit_length()))) % 2
            pieces.append(jnp.where(want == 0, low, high))
        return jnp.concatenate(pieces, axis=0)

    other_block = across(batch, spread[0])
    other_centers = swap(centers, total, core)
    other_weights = swap(weights, total, core)
    rows = jnp.concatenate([chosen(batch, 0), chosen(other_block, 1)], axis=0)
    for pair in spread[1:-1]:
        rows = jnp.concatenate([rows, across(rows, pair)], axis=0)
    rows, other_centers, other_weights = lax.optimization_barrier((rows, other_centers, other_weights))
    far_rows = across(rows, spread[-1])

    mine = (jnp.arange(lead) // own_rows == seat)[:, None]
    taken = jnp.where(mine, jnp.tile(targets, (seats, 1)), 0.0)
    operands = (centers, other_centers, weights, other_weights)
    early, early_kernel, norms = early_half(rows, taken, pred_scale, *operands)
    value, kernel, other_kernel = late_half(far_rows, early, early_kernel, norms, pred_scale, *operands)
    swapped = swap(other_kernel, total, core)

    for pair in zip(line, other_line):
        got = across(value, pair)
        turns = [order.index(m) if m in order else None for m, order in zip(pair, (first, second))]
        here, there = (flipped(got, turn, lead) for turn in turns)
        value = value + (here if turns[0] == turns[1] else jnp.where(parity == 0, here, there))
    residual = lax.dynamic_slice_in_dim(value, seat * own_rows, own_rows, axis=0)
    partner = swap(value, total, core)

    def change(kernel, values):
        return lax.dot_general(
            kernel, values, (((0,), (0,)), ((), ())), precision=HIGHEST, preferred_element_type=jnp.float32
        )

    rate = 32.0 / all_rows
    new_weights = weights - rate * change(kernel, value) - rate * change(swapped, partner)
    return (residual, new_weights)


def solution(mesh):
    return jax.shard_map(
        shards,
        mesh=mesh,
        in_specs=(
            P("wide", None),
            P(("wide", "narrow"), None),
            P(("wide", "narrow"), None),
            P(("wide", "narrow"), None),
        ),
        out_specs=(P(("wide", "narrow"), None), P(("wide", "narrow"), None)),
        check_vma=False,
    )
```

time: 44.5 us -> 39.5 us (0.89)
  Pallas kernels: 0 us -> 2.82 us
  waiting for transfers between devices: 16.7 us -> 14 us
  matrix products: 3.32 us -> 1.55 us
  starting transfers between devices: 20.1 us -> 18.5 us
  other arithmetic: 1.5 us -> 0.21 us
    pallas_call x0 -> x2, Pallas kernels: none -> 2.82 us  [call(): pl.pallas_call(body, out_shape=[jax.ShapeDtypeStruct(shape, jnp.float32)...]
    ppermute x12 -> x11, waiting for transfers between devices: 16.7 us -> 14 us  [swap(): lax.ppermute(value, AXES, [(i, i ^ masks[odd(i)]) for i in range(total)])]
    dot_general x6 -> x2, matrix products: 3.32 us -> 1.55 us  [change(): lax.dot_general(kernel, values, (((0,), (0,)), ((), ())), precision=HIGHE...]
    ppermute x12 -> x11, starting transfers between devices: 20.1 us -> 18.5 us  [swap(): lax.ppermute(value, AXES, [(i, i ^ masks[odd(i)]) for i in range(total)])]
    reduce_sum x3 -> x0, other arithmetic: 1.34 us -> none  [the longest x2 1.23 us: block(): norms = jnp.sum(points * points, axis=1)]
    reshape x1 -> x0, local copies, waits for them, and re-layouts: 0.82 us -> none  [shards(): paired = batch.reshape(seats, 2, own_rows, features)]
    another operation x2, local copies, waits for them, and re-layouts: 0.01 us -> 0.71 us  [shards(): taken = jnp.where(mine, jnp.tile(targets, (seats, 1)), 0.0)]
  transfers between devices with their start and end apart: 12 -> 11, of which waited for: 9 -> 8; matrix products, arithmetic and copies ran while one was open for 8% -> 4% of each run, Pallas kernels for 0% -> 4%
where the time goes in v2:
time: 39.5 us; the launch traced here: 39.3 us
  starting transfers between devices  18.5 us (47%)
  waiting for transfers between devices  14 us (35%)
  Pallas kernels  2.82 us (7%)
  matrix products  1.55 us (4%)
  local copies, waits for them, and re-layouts  1.43 us (4%)
  between operations  0.79 us (2%)
    ppermute x11, starting transfers between devices, swap(): lax.ppermute(value, AXES, [(i, i ^ masks[odd(i)]) for i in range(total)])  18.5 us
    ppermute x11, waiting for transfers between devices, swap(): lax.ppermute(value, AXES, [(i, i ^ masks[odd(i)]) for i in range(total)])  14 us
    pallas_call x2, Pallas kernels, call(): pl.pallas_call(body, out_shape=[jax.ShapeDtypeStruct(shape, jnp.float32)...  2.82 us
    dot_general x2, matrix products, change(): lax.dot_general(kernel, values, (((0,), (0,)), ((), ())), precision=HIGHE...  1.55 us
  transfers between devices with their start and end apart: 11, of which 8 were waited for; matrix products, arithmetic and copies ran while one was open for 4% of the time, Pallas kernels for 4%

profile of v2, /device:TPU:0, one launch (start us, length us, event | category | flops | bytes accessed | tf_op | source)
XLA Modules:
  0.0 39.3 jit_solution(8311535215305676943)
XLA Ops:
  0.6 0.0 copy-start.2
  0.6 0.0 copy-start.1
  0.6 2.5 %collective-permute-start = (f32[16,768]{1,0:T(8,128)}, f32[16,768]{1,0:T(8,128)S(1)}, u32[]{:S(2)}, u32[]{:S(2)}) collective-permute-start(f32[16,768]{1,0:T(8,128)} %param.4), channel_id=1, source_target_pairs={{0,5},{1,16},{2,19},{3,6},{4,21},{5,0},{6,3},{7,22},{8,25},{9,12},... | collective-permute-start | bytes 147464 | tf_op jit(solution)/shard_map/ppermute | solution.py:20
  3.1 1.8 %collective-permute-start.3 = (f32[128,512]{1,0:T(8,128)}, f32[128,512]{1,0:T(8,128)S(1)}, u32[]{:S(2)}, u32[]{:S(2)}) collective-permute-start(f32[128,512]{1,0:T(8,128)} %weights.3), channel_id=1, source_target_pairs={{0,1},{1,0},{2,3},{3,2},{4,5},{5,4},{6,7},{7,6},{8,9},{9,8},{10,11... | collective-permute-start | bytes 786440 | tf_op jit(solution)/shard_map/ppermute | solution.py:20
  4.9 0.0 collective-permute-start.2
  4.9 0.0 copy-done.2
  4.9 0.0 copy-start
  5.0 0.2 collective-permute-done
  5.2 2.9 %collective-permute-start.1 = (f32[16,768]{1,0:T(8,128)S(1)}, f32[16,768]{1,0:T(8,128)S(1)}, u32[]{:S(2)}, u32[]{:S(2)}) collective-permute-start(f32[16,768]{1,0:T(8,128)S(1)} %pad_maximum_fusion), channel_id=1, source_target_pairs={{0,17},{1,8},{2,11},{3,18},{4,13},{5,20},{6,23},{7,14},{8,1},{9,24... | collective-permute-start | bytes 147464 | tf_op jit(solution)/shard_map/ppermute | solution.py:20
  8.1 0.7 %tile.4 = f32[2,4,512]{2,1,0:T(4,128)S(1)} broadcast(f32[4,512]{1,0:T(4,128)} %param.5), dimensions={1,2} | broadcast | bytes 24576 | tf_op jit(solution)/shard_map/tile | solution.py:153
  8.8 1.3 %collective-permute-done.1 = f32[16,768]{1,0:T(8,128)S(1)} collective-permute-done((f32[16,768]{1,0:T(8,128)S(1)}, f32[16,768]{1,0:T(8,128)S(1)}, u32[]{:S(2)}, u32[]{:S(2)}) %collective-permute-start.1) | collective-permute-done | bytes 49184 | tf_op jit(solution)/shard_map/ppermute | solution.py:20
  10.1 0.1 concatenate.8.rows
  10.1 0.0 collective-permute-done.3.other_weights
  10.1 0.0 collective-permute-done.2.other_centers
  10.1 1.7 %collective-permute-start.4 = (f32[32,768]{1,0:T(8,128)S(1)}, f32[32,768]{1,0:T(8,128)S(1)}, u32[]{:S(2)}, u32[]{:S(2)}) collective-permute-start(f32[32,768]{1,0:T(8,128)S(1)} %concatenate.8.rows), channel_id=1, source_target_pairs={{0,9},{1,4},{2,7},{3,10},{4,1},{5,12},{6,15},{7,2},{8,13},{9,0},{1... | collective-permute-start | bytes 294920 | tf_op jit(solution)/shard_map/ppermute | solution.py:20
  11.8 0.1 broadcast_select_fusion.taken
  11.9 0.0 copy-done.1
  11.9 0.0 copy-done
  11.9 1.7 %shard_map.59 = (f32[32,512]{1,0:T(8,128)S(1)}, f32[32,256]{1,0:T(8,128)S(1)}, f32[1,256]{1,0:T(1,128)S(1)}) custom-call(f32[32,768]{1,0:T(8,128)S(1)} %concatenate.8.rows, f32[8,512]{1,0:T(8,128)S(1)} %broadcast_select_fusion.taken, f32[128,768]{1,0:T(8,128)S(1)} %copy-done.1, f32[128,768]{1,0:T(8,128)S(1)} %collective-permute-done.2.other_centers, ...), custom_call_target="tpu_custom_call" | custom-call | tf_op jit(solution)/shard_map/pallas_call | solution.py:76
  13.6 0.7 %collective-permute-done.4.rows = f32[32,768]{1,0:T(8,128)S(1)} collective-permute-done((f32[32,768]{1,0:T(8,128)S(1)}, f32[32,768]{1,0:T(8,128)S(1)}, u32[]{:S(2)}, u32[]{:S(2)}) %collective-permute-start.4) | collective-permute-done | bytes 98336 | tf_op jit(solution)/shard_map/ppermute | solution.py:20
  14.2 1.2 %shard_map.60 = (f32[64,512]{1,0:T(8,128)S(1)}, f32[64,128]{1,0:T(8,128)S(1)}, f32[64,128]{1,0:T(8,128)S(1)}) custom-call(f32[32,768]{1,0:T(8,128)S(1)} %collective-permute-done.4.rows, f32[32,512]{1,0:T(8,128)S(1)} %get-tuple-element.14.early, f32[32,256]{1,0:T(8,128)S(1)} %get-tuple-element.15.early_kernel, f32[1,256]{1,0:T(1,128)S(1)} %get-tuple-element.16.norms, ...), custom_call_target="tpu_custom_call" | custom-call | tf_op jit(solution)/shard_map/pallas_call | solution.py:76
  15.4 2.0 %collective-permute-start.5 = (f32[64,512]{1,0:T(8,128)S(1)}, f32[64,512]{1,0:T(8,128)S(1)}, u32[]{:S(2)}, u32[]{:S(2)}) collective-permute-start(f32[64,512]{1,0:T(8,128)S(1)} %get-tuple-element.17), channel_id=1, source_target_pairs={{0,3},{1,16},{2,19},{3,0},{4,21},{5,6},{6,5},{7,22},{8,25},{9,10},... | collective-permute-start | bytes 393224 | tf_op jit(solution)/shard_map/ppermute | solution.py:20
  17.4 2.7 %collective-permute-done.5 = f32[64,512]{1,0:T(8,128)S(1)} collective-permute-done((f32[64,512]{1,0:T(8,128)S(1)}, f32[64,512]{1,0:T(8,128)S(1)}, u32[]{:S(2)}, u32[]{:S(2)}) %collective-permute-start.5) | collective-permute-done | bytes 131104 | tf_op jit(solution)/shard_map/ppermute | solution.py:20
  20.1 3.2 %collective-permute-start.6 = (f32[64,512]{1,0:T(8,128)S(1)}, f32[64,512]{1,0:T(8,128)S(1)}, u32[]{:S(2)}, u32[]{:S(2)}) collective-permute-start(f32[64,512]{1,0:T(8,128)S(1)} %fusion.4), channel_id=1, source_target_pairs={{0,17},{1,2},{2,1},{3,18},{4,7},{5,20},{6,23},{7,4},{8,11},{9,24},... | collective-permute-start | bytes 393224 | tf_op jit(solution)/shard_map/ppermute | solution.py:20
  23.3 2.7 %collective-permute-done.6 = f32[64,512]{1,0:T(8,128)S(1)} collective-permute-done((f32[64,512]{1,0:T(8,128)S(1)}, f32[64,512]{1,0:T(8,128)S(1)}, u32[]{:S(2)}, u32[]{:S(2)}) %collective-permute-start.6) | collective-permute-done | bytes 131104 | tf_op jit(solution)/shard_map/ppermute | solution.py:20
  26.0 3.0 %collective-permute-start.7 = (f32[64,512]{1,0:T(8,128)S(1)}, f32[64,512]{1,0:T(8,128)S(1)}, u32[]{:S(2)}, u32[]{:S(2)}) collective-permute-start(f32[64,512]{1,0:T(8,128)S(1)} %fusion.3), channel_id=1, source_target_pairs={{0,5},{1,8},{2,11},{3,6},{4,13},{5,0},{6,3},{7,14},{8,1},{9,12},{1... | collective-permute-start | bytes 393224 | tf_op jit(solution)/shard_map/ppermute | solution.py:20
  29.0 2.7 %collective-permute-done.7 = f32[64,512]{1,0:T(8,128)S(1)} collective-permute-done((f32[64,512]{1,0:T(8,128)S(1)}, f32[64,512]{1,0:T(8,128)S(1)}, u32[]{:S(2)}, u32[]{:S(2)}) %collective-permute-start.7) | collective-permute-done | bytes 131104 | tf_op jit(solution)/shard_map/ppermute | solution.py:20
  31.7 1.0 %collective-permute-start.8 = (f32[64,512]{1,0:T(8,128)S(1)}, f32[64,512]{1,0:T(8,128)S(1)}, u32[]{:S(2)}, u32[]{:S(2)}) collective-permute-start(f32[64,512]{1,0:T(8,128)S(1)} %fusion.2), channel_id=1, source_target_pairs={{0,9},{1,4},{2,7},{3,10},{4,1},{5,12},{6,15},{7,2},{8,13},{9,0},{1... | collective-permute-start | bytes 393224 | tf_op jit(solution)/shard_map/ppermute | solution.py:20
  32.7 3.5 %collective-permute-done.8 = f32[64,512]{1,0:T(8,128)S(1)} collective-permute-done((f32[64,512]{1,0:T(8,128)S(1)}, f32[64,512]{1,0:T(8,128)S(1)}, u32[]{:S(2)}, u32[]{:S(2)}) %collective-permute-start.8) | collective-permute-done | bytes 131104 | tf_op jit(solution)/shard_map/ppermute | solution.py:20
  36.2 0.3 collective-permute-start.10
  36.5 0.2 collective-permute-start.9
  36.8 0.6 %constant_dynamic-slice_fusion = f32[4,512]{1,0:T(4,128)} fusion(f32[64,512]{1,0:T(8,128)S(1)} %bitcast_add_fusion, s32[]{:T(128)S(6)} %select_n.110), kind=kLoop, calls=%fused_computation.22 | loop fusion | bytes 16388 | tf_op jit(solution)/shard_map/dynamic_slice | solution.py:164
  37.4 0.4 collective-permute-done.9
  37.8 0.0 collective-permute-done.10
  37.8 0.4 %convolution_multiply_fusion = f32[128,512]{1,0:T(8,128)S(1)} fusion(f32[64,128]{1,0:T(8,128)S(1)} %collective-permute-done.9, f32[64,512]{1,0:T(8,128)S(1)} %collective-permute-done.10), kind=kOutput, calls=%fused_computation | convolution fusion | flops 50397184 | bytes 425984 | tf_op jit(solution)/shard_map/dot_general | solution.py:168
  38.2 1.1 %fusion.1 = f32[128,512]{1,0:T(8,128)} fusion(f32[128,512]{1,0:T(8,128)S(1)} %convolution_multiply_fusion, f32[128,512]{1,0:T(8,128)S(1)} %copy-done, f32[64,128]{1,0:T(8,128)S(1)} %get-tuple-element.18, f32[64,512]{1,0:T(8,128)S(1)} %bitcast_add_fusion), kind=kOutput, calls=%fused_computation.3 | convolution fusion | flops 50528256 | bytes 950272 | tf_op jit(solution)/shard_map/dot_general | solution.py:168
  (14 shorter events, 0.2 us)
Async XLA Ops:
  0.6 4.3 %copy-start.2 = (f32[16,768]{1,0:T(8,128)S(1)}, f32[16,768]{1,0:T(8,128)}, u32[]{:S(2)}) copy-start(f32[16,768]{1,0:T(8,128)} %param.4) | copy-start | bytes 147460
  0.6 11.3 %copy-start.1 = (f32[128,768]{1,0:T(8,128)S(1)}, f32[128,768]{1,0:T(8,128)}, u32[]{:S(2)}) copy-start(f32[128,768]{1,0:T(8,128)} %centers.3) | copy-start | bytes 1179652
  0.6 4.5 %collective-permute-start = (f32[16,768]{1,0:T(8,128)}, f32[16,768]{1,0:T(8,128)S(1)}, u32[]{:S(2)}, u32[]{:S(2)}) collective-permute-start(f32[16,768]{1,0:T(8,128)} %param.4), channel_id=1, source_target_pairs={{0,5},{1,16},{2,19},{3,6},{4,21},{5,0},{6,3},{7,22},{8,25},{9,12},... | collective-permute-start | bytes 147464 | tf_op jit(solution)/shard_map/ppermute | solution.py:20
  3.1 7.0 %collective-permute-start.3 = (f32[128,512]{1,0:T(8,128)}, f32[128,512]{1,0:T(8,128)S(1)}, u32[]{:S(2)}, u32[]{:S(2)}) collective-permute-start(f32[128,512]{1,0:T(8,128)} %weights.3), channel_id=1, source_target_pairs={{0,1},{1,0},{2,3},{3,2},{4,5},{5,4},{6,7},{7,6},{8,9},{9,8},{10,11... | collective-permute-start | bytes 786440 | tf_op jit(solution)/shard_map/ppermute | solution.py:20
  4.9 5.2 %collective-permute-start.2 = (f32[128,768]{1,0:T(8,128)}, f32[128,768]{1,0:T(8,128)S(1)}, u32[]{:S(2)}, u32[]{:S(2)}) collective-permute-start(f32[128,768]{1,0:T(8,128)} %centers.3), channel_id=1, source_target_pairs={{0,1},{1,0},{2,3},{3,2},{4,5},{5,4},{6,7},{7,6},{8,9},{9,8},{10,11... | collective-permute-start | bytes 1179656 | tf_op jit(solution)/shard_map/ppermute | solution.py:20
  4.9 7.0 %copy-start = (f32[128,512]{1,0:T(8,128)S(1)}, f32[128,512]{1,0:T(8,128)}, u32[]{:S(2)}) copy-start(f32[128,512]{1,0:T(8,128)} %weights.3) | copy-start | bytes 786436
  5.2 4.8 %collective-permute-start.1 = (f32[16,768]{1,0:T(8,128)S(1)}, f32[16,768]{1,0:T(8,128)S(1)}, u32[]{:S(2)}, u32[]{:S(2)}) collective-permute-start(f32[16,768]{1,0:T(8,128)S(1)} %pad_maximum_fusion), channel_id=1, source_target_pairs={{0,17},{1,8},{2,11},{3,18},{4,13},{5,20},{6,23},{7,14},{8,1},{9,24... | collective-permute-start | bytes 147464 | tf_op jit(solution)/shard_map/ppermute | solution.py:20
  10.1 4.1 %collective-permute-start.4 = (f32[32,768]{1,0:T(8,128)S(1)}, f32[32,768]{1,0:T(8,128)S(1)}, u32[]{:S(2)}, u32[]{:S(2)}) collective-permute-start(f32[32,768]{1,0:T(8,128)S(1)} %concatenate.8.rows), channel_id=1, source_target_pairs={{0,9},{1,4},{2,7},{3,10},{4,1},{5,12},{6,15},{7,2},{8,13},{9,0},{1... | collective-permute-start | bytes 294920 | tf_op jit(solution)/shard_map/ppermute | solution.py:20
  15.4 4.7 %collective-permute-start.5 = (f32[64,512]{1,0:T(8,128)S(1)}, f32[64,512]{1,0:T(8,128)S(1)}, u32[]{:S(2)}, u32[]{:S(2)}) collective-permute-start(f32[64,512]{1,0:T(8,128)S(1)} %get-tuple-element.17), channel_id=1, source_target_pairs={{0,3},{1,16},{2,19},{3,0},{4,21},{5,6},{6,5},{7,22},{8,25},{9,10},... | collective-permute-start | bytes 393224 | tf_op jit(solution)/shard_map/ppermute | solution.py:20
  20.1 5.8 %collective-permute-start.6 = (f32[64,512]{1,0:T(8,128)S(1)}, f32[64,512]{1,0:T(8,128)S(1)}, u32[]{:S(2)}, u32[]{:S(2)}) collective-permute-start(f32[64,512]{1,0:T(8,128)S(1)} %fusion.4), channel_id=1, source_target_pairs={{0,17},{1,2},{2,1},{3,18},{4,7},{5,20},{6,23},{7,4},{8,11},{9,24},... | collective-permute-start | bytes 393224 | tf_op jit(solution)/shard_map/ppermute | solution.py:20
  26.0 5.7 %collective-permute-start.7 = (f32[64,512]{1,0:T(8,128)S(1)}, f32[64,512]{1,0:T(8,128)S(1)}, u32[]{:S(2)}, u32[]{:S(2)}) collective-permute-start(f32[64,512]{1,0:T(8,128)S(1)} %fusion.3), channel_id=1, source_target_pairs={{0,5},{1,8},{2,11},{3,6},{4,13},{5,0},{6,3},{7,14},{8,1},{9,12},{1... | collective-permute-start | bytes 393224 | tf_op jit(solution)/shard_map/ppermute | solution.py:20
  31.7 4.5 %collective-permute-start.8 = (f32[64,512]{1,0:T(8,128)S(1)}, f32[64,512]{1,0:T(8,128)S(1)}, u32[]{:S(2)}, u32[]{:S(2)}) collective-permute-start(f32[64,512]{1,0:T(8,128)S(1)} %fusion.2), channel_id=1, source_target_pairs={{0,9},{1,4},{2,7},{3,10},{4,1},{5,12},{6,15},{7,2},{8,13},{9,0},{1... | collective-permute-start | bytes 393224 | tf_op jit(solution)/shard_map/ppermute | solution.py:20
  36.2 1.6 %collective-permute-start.10 = (f32[64,512]{1,0:T(8,128)S(1)}, f32[64,512]{1,0:T(8,128)S(1)}, u32[]{:S(2)}, u32[]{:S(2)}) collective-permute-start(f32[64,512]{1,0:T(8,128)S(1)} %bitcast_add_fusion), channel_id=1, source_target_pairs={{0,1},{1,0},{2,3},{3,2},{4,5},{5,4},{6,7},{7,6},{8,9},{9,8},{10,11... | collective-permute-start | bytes 393224 | tf_op jit(solution)/shard_map/ppermute | solution.py:20
  36.5 1.2 %collective-permute-start.9 = (f32[64,128]{1,0:T(8,128)S(1)}, f32[64,128]{1,0:T(8,128)S(1)}, u32[]{:S(2)}, u32[]{:S(2)}) collective-permute-start(f32[64,128]{1,0:T(8,128)S(1)} %get-tuple-element.19), channel_id=1, source_target_pairs={{0,1},{1,0},{2,3},{3,2},{4,5},{5,4},{6,7},{7,6},{8,9},{9,8},{10,11... | collective-permute-start | bytes 98312 | tf_op jit(solution)/shard_map/ppermute | solution.py:20
